TPU v7x, 32 devices: a whole 2x2x4 slice. The times are simulated.
32 devices in a mesh: groups: 2 (over x), space: 8 (over z, y), beam: 2 (over core).
Axes of the slice: x: 2, y: 2, z: 4, core: 2. Of those that a mesh axis runs over, the one named last changes fastest.
Arguments:
- s_matrix: bfloat16 [4096, 256, 480], P(('groups', 'beam'), 'space'), parts along dimension 0, may hold values from -6 to 6
- beam_index: int32 [2048, 2], P('beam'), may hold values from -24 to 23, as said below
- beam_amp: float32 [2048], P('beam'), may hold values from 0.5 to 2
- beam_phase: float32 [2048], P('beam'), may hold values from -3.140625 to 3.140625
- positions: int32 [2, 384, 2], replicated, may hold values from 0 to 239
Outputs:
- intensities: float32 [4, 384, 256, 240], P('groups', ('space', 'beam')), parts along dimension 0
There are 2 independent parts, one for each index of `groups`. A program takes and returns all parts, laid end to end along the dimension named above; an argument that names none is the same for every part. Nothing has to cross between parts.
Inputs may be any that keep to these rules, and one draw needn't show every extreme that they name: `beam_index`: no two beams have the same wave-vector.
All inputs are finite; a program needn't handle non-finite values.
Results may differ from a plain program's by a relative error of at most 0.0072.
Values may be sent and summed in bfloat16 or wider, within the bound.
No kernel may reach another device: no remote copies, remote signals or barrier semaphores. Data moves between devices by JAX's collectives and lax.ppermute only.
A program may use at most 192 MiB of HBM per device.

v0:
```python
import math
import jax
import jax.numpy as jnp
from jax import lax
from jax.sharding import PartitionSpec as P

NB = 2048
RY = 256
RX = 240


def dft_tables():
    xs = jnp.arange(RX, dtype=jnp.int32)
    prod_x = jnp.mod(xs[:, None] * xs[None, :], RX).astype(jnp.float32)
    angle_x = 2.0 * math.pi / RX * prod_x
    cos_x = jnp.cos(angle_x) / math.sqrt(RX)
    sin_x = jnp.sin(angle_x) / math.sqrt(RX)
    table_x = jnp.concatenate(
        [jnp.concatenate([cos_x, -sin_x], 1), jnp.concatenate([sin_x, cos_x], 1)], 0
    ).astype(jnp.bfloat16)
    ys = jnp.arange(RY, dtype=jnp.int32)
    prod_y = jnp.mod(ys[:, None] * ys[None, :], RY).astype(jnp.float32)
    angle_y = 2.0 * math.pi / RY * prod_y
    table_y = jnp.concatenate([jnp.cos(angle_y), jnp.sin(angle_y)], 0) / math.sqrt(RY)
    return (table_x, table_y.astype(jnp.bfloat16))


def coefficients(spots, beam_index, beam_amp, beam_phase):
    rows_part = jnp.mod(spots[:, 0:1] * beam_index[None, :, 0], RY).astype(jnp.float32)
    cols_part = jnp.mod(spots[:, 1:2] * beam_index[None, :, 1], RX).astype(jnp.float32)
    theta = beam_phase[None, :] - 2.0 * math.pi * (rows_part / RY + cols_part / RX)
    scale = beam_amp[None, :] / math.sqrt(NB)
    return (
        (scale * jnp.cos(theta)).astype(jnp.bfloat16),
        (scale * jnp.sin(theta)).astype(jnp.bfloat16),
    )


def body(s_matrix, beam_index, beam_amp, beam_phase, positions):
    local_beams = s_matrix.shape[0]
    local_rows = s_matrix.shape[1]
    n_space = lax.axis_size("space")
    n_beam = lax.axis_size("beam")
    n_batch = positions.shape[0]
    per_device = positions.shape[1] // (n_space * n_beam)
    flat_s = s_matrix.reshape(local_beams, local_rows * 2 * RX)
    table_x, table_y = dft_tables()

    def transform(wave, count):
        half = jnp.dot(wave.reshape(-1, 2 * RX), table_x, preferred_element_type=jnp.float32)
        half = half.astype(jnp.bfloat16).reshape(-1, RY, 2 * RX)
        spectrum = jnp.einsum("vy,pyc->pvc", table_y, half, preferred_element_type=jnp.float32)
        spec_re = spectrum[:, :RY, :RX] + spectrum[:, RY:, RX:]
        spec_im = spectrum[:, :RY, RX:] - spectrum[:, RY:, :RX]
        return (spec_re * spec_re + spec_im * spec_im).reshape(count, per_device, RY, RX)

    def one_group(chosen):
        count = chosen.shape[0]
        blocks = chosen.reshape(count, n_space, n_beam, per_device, 2)
        spots = jnp.transpose(blocks, (2, 1, 0, 3, 4)).reshape(-1, 2)
        coef_re, coef_im = coefficients(spots, beam_index, beam_amp, beam_phase)
        total_rows = spots.shape[0]
        product = jnp.dot(
            jnp.concatenate([coef_re, coef_im], 0), flat_s, preferred_element_type=jnp.float32
        )
        product = product.reshape(
            2, total_rows // n_beam * lax.axis_size("beam"), local_rows, 2 * RX
        )
        wave_re = product[0, ..., :RX] - product[1, ..., RX:]
        wave_im = product[0, ..., RX:] + product[1, ..., :RX]
        rounded = lax.optimization_barrier(
            jnp.concatenate([wave_re, wave_im], -1).astype(jnp.bfloat16)
        )
        summed = lax.psum_scatter(
            rounded.astype(jnp.float32).astype(jnp.bfloat16),
            "beam",
            scatter_dimension=0,
            tiled=True,
        )
        wave = lax.all_to_all(summed, "space", split_axis=0, concat_axis=1, tiled=True)
        return transform(wave, count)

    outputs = [one_group(positions[batch : batch + 1]) for batch in range(n_batch)]
    return jnp.concatenate(outputs, 0)


def solution(mesh):
    in_specs = (P(("groups", "beam"), "space", None), P("beam", None), P("beam"), P("beam"), P())
    out_specs = P("groups", ("space", "beam"), None, None)
    return jax.shard_map(body, mesh=mesh, in_specs=in_specs, out_specs=out_specs, check_vma=False)
```

profile of v0, /device:TPU:0, one launch (start us, length us, event | category | flops | bytes accessed | tf_op | source)
XLA Modules:
  0.0 513.1 jit_solution(4622857411658525311)
XLA Ops:
  6.5 0.0 reduce-scatter.5.cloned.1.call-start
  6.5 0.7 broadcast_multiply_fusion
  7.2 0.7 fusion.71
  7.9 0.8 fusion.70
  8.7 0.1 reshape.54
  8.8 0.1 reshape.55
  8.9 0.1 reshape.60
  9.1 0.1 reshape.61
  9.2 16.0 %multiply_convert_fusion.3 = (bf16[384,1024]{1,0:T(8,128)(2,1)S(1)}, bf16[384,1024]{1,0:T(8,128)(2,1)S(1)}, bf16[384,1024]{1,0:T(8,128)(2,1)S(1)}, bf16[384,1024]{1,0:T(8,128)(2,1)S(1)}) fusion(s32[1024]{0:T(1024)S(1)} %bitcast.92, s32[384]{0:T(512)S(1)} %get-tuple-element.6, s32[1024]{0:T(1024)S(1)} %bitcast.91, s32[384]{0:T(512)S(1)} %get-tuple-element.5, ...), kind=kLoop, calls=%fused_computation.75 | loop fusion | flops 23592960 | bytes 3168256 | tf_op jit(solution)/shard_map/convert_element_type | solution.py:34
  25.2 1.5 pad_maximum_fusion.3
  26.7 34.1 %fusion = f32[2,384,32,480]{1,3,2,0:T(8,128)} fusion(bf16[2,384,1024,1]{2,1,3,0:T(8,128)(2,1)S(1)} %bitcast.88, bf16[1024,32,480]{0,2,1:T(8,128)(2,1)} %param.5), kind=kOutput, calls=%fused_computation | convolution fusion | flops 24159191040 | bytes 80216064 | tf_op jit(solution)/shard_map/dot_general | solution.py:63
  60.7 15.8 %fusion.10 = (bf16[384,32,240]{0,2,1:T(8,128)(2,1)S(1)}, bf16[384,32,240]{0,2,1:T(8,128)(2,1)S(1)}) fusion(f32[2,384,32,480]{1,3,2,0:T(8,128)} %fusion), kind=kLoop, calls=%fused_computation.21 | loop fusion | flops 11796480 | bytes 58982400 | tf_op jit(solution)/shard_map/sub | solution.py:69
  76.6 5.5 %pad_maximum_fusion.1 = bf16[384,32,480]{0,2,1:T(8,128)(2,1)} fusion(bf16[384,32,240]{0,2,1:T(8,128)(2,1)S(1)} %get-tuple-element.12, bf16[384,32,240]{0,2,1:T(8,128)(2,1)S(1)} %get-tuple-element.11), kind=kLoop, calls=%fused_computation.13 | loop fusion | flops 23592960 | bytes 23592960 | tf_op jit(solution)/shard_map/concatenate | solution.py:72
  82.1 16.8 %copy.21 = bf16[384,32,480]{2,1,0:T(8,128)(2,1)} copy(bf16[384,32,480]{0,2,1:T(8,128)(2,1)} %pad_maximum_fusion.1) | data formatting | bytes 23592960 | tf_op jit(solution)/shard_map/optimization_barrier | solution.py:71
  98.8 0.0 copy-start
  98.8 0.0 reduce-scatter.5.cloned.1.call-update
  98.8 0.2 reduce-scatter.3.cloned.1.call-start
  99.1 1.2 copy-done
  100.2 35.8 %fusion.2 = f32[2,384,32,480]{1,3,2,0:T(8,128)} fusion(bf16[2,384,1024,1]{2,1,3,0:T(8,128)(2,1)S(1)} %bitcast.87, bf16[1024,32,480]{0,2,1:T(8,128)(2,1)} %param.5), kind=kOutput, calls=%fused_computation.2 | convolution fusion | flops 24159191040 | bytes 80216064 | tf_op jit(solution)/shard_map/dot_general | solution.py:63
  136.0 15.8 %fusion.8 = (bf16[384,32,240]{0,2,1:T(8,128)(2,1)S(1)}, bf16[384,32,240]{0,2,1:T(8,128)(2,1)S(1)}) fusion(f32[2,384,32,480]{1,3,2,0:T(8,128)} %fusion.2), kind=kLoop, calls=%fused_computation.19 | loop fusion | flops 11796480 | bytes 58982400 | tf_op jit(solution)/shard_map/sub | solution.py:69
  151.8 5.5 %pad_maximum_fusion = bf16[384,32,480]{0,2,1:T(8,128)(2,1)} fusion(bf16[384,32,240]{0,2,1:T(8,128)(2,1)S(1)} %get-tuple-element.10, bf16[384,32,240]{0,2,1:T(8,128)(2,1)S(1)} %get-tuple-element.9), kind=kLoop, calls=%fused_computation.12 | loop fusion | flops 23592960 | bytes 23592960 | tf_op jit(solution)/shard_map/concatenate | solution.py:72
  157.3 16.6 %copy.17 = bf16[384,32,480]{2,1,0:T(8,128)(2,1)} copy(bf16[384,32,480]{0,2,1:T(8,128)(2,1)} %pad_maximum_fusion) | data formatting | bytes 23592960 | tf_op jit(solution)/shard_map/optimization_barrier | solution.py:71
  173.9 0.0 reduce-scatter.3.cloned.1.call-update
  174.0 0.0 reduce-scatter.5.cloned.1.call-done
  174.0 7.6 %all-to-all-start.1 = ((bf16[192,32,480]{2,1,0:T(8,128)(2,1)}), bf16[192,32,480]{2,1,0:T(8,128)(2,1)}, u32[]{:S(2)}, u32[]{:S(2)}) async-start(bf16[192,32,480]{2,1,0:T(8,128)(2,1)} %reduce-scatter.5.cloned.1.call-done), calls=%async_computation.3 | async-start | bytes 12582912 | tf_op jit(solution)/shard_map/all_to_all | solution.py:80
  181.6 16.3 %reduce-scatter.3.cloned.1.call-done = bf16[192,32,480]{2,1,0:T(8,128)(2,1)} async-done(((bf16[384,32,480]{2,1,0:T(8,128)(2,1)}), bf16[192,32,480]{2,1,0:T(8,128)(2,1)}) %reduce-scatter.3.cloned.1.call-update) | async-done | bytes 5898256 | tf_op jit(solution)/shard_map/reduce_scatter | solution.py:74
  197.9 121.8 %all-to-all-done.1 = bf16[192,32,480]{2,1,0:T(8,128)(2,1)} async-done(((bf16[192,32,480]{2,1,0:T(8,128)(2,1)}), bf16[192,32,480]{2,1,0:T(8,128)(2,1)}, u32[]{:S(2)}, u32[]{:S(2)}) %all-to-all-start.1) | async-done | bytes 5898272 | tf_op jit(solution)/shard_map/all_to_all | solution.py:80
  319.7 5.0 all-to-all-start
  324.7 1.0 fusion.59
  325.6 1.1 negate_convert_fusion
  326.7 1.0 fusion.60
  327.8 3.4 copy.22
  331.2 4.0 convolution_convert_fusion
  335.2 9.6 %convolution_bitcast_fusion = f32[24,512,480]{1,2,0:T(8,128)} fusion(bf16[60,24,8,256]{3,2,1,0:T(8,128)(2,1)S(1)} %bitcast.82, f32[256,256]{1,0:T(8,128)S(1)} %get-tuple-element.27, f32[256,256]{1,0:T(8,128)S(1)} %get-tuple-element.28), kind=kOutput, calls=%fused_computation.17 | convolution fusion | flops 3020292096 | bytes 30015488 | tf_op jit(solution)/shard_map/vy,pyc->pvc/dot_general | solution.py:52
  344.8 11.4 %fusion.18 = f32[1,24,256,240]{2,3,1,0:T(8,128)} fusion(f32[24,512,480]{1,2,0:T(8,128)} %convolution_bitcast_fusion), kind=kLoop, calls=%fused_computation.30 | loop fusion | flops 7372800 | bytes 29491200 | tf_op jit(solution)/shard_map/reshape | solution.py:55
  356.2 105.5 %all-to-all-done = bf16[192,32,480]{2,1,0:T(8,128)(2,1)} async-done(((bf16[192,32,480]{2,1,0:T(8,128)(2,1)}), bf16[192,32,480]{2,1,0:T(8,128)(2,1)}, u32[]{:S(2)}, u32[]{:S(2)}) %all-to-all-start) | async-done | bytes 5898272 | tf_op jit(solution)/shard_map/all_to_all | solution.py:80
  461.7 6.6 %copy.18 = bf16[24,8,32,480]{3,2,1,0:T(8,128)(2,1)} copy(bf16[24,8,32,480]{3,2,0,1:T(8,128)(2,1)} %bitcast.13) | data formatting | bytes 11796480 | tf_op jit(solution)/shard_map/all_to_all | solution.py:80
  468.3 0.0 slice-start
  468.3 8.7 %convolution_convert_fusion.1 = bf16[6144,480]{0,1:T(8,128)(2,1)S(1)} fusion(bf16[6144,480]{1,0:T(8,128)(2,1)} %bitcast.85, bf16[240,240]{1,0:T(8,128)(2,1)S(1)} %get-tuple-element.26, bf16[240,240]{1,0:T(8,128)(2,1)S(1)} %fusion.59, bf16[240,240]{1,0:T(8,128)(2,1)S(1)} %get-tuple-element.25), kind=kOutput, calls=%fused_computation.16 | convolution fusion | flops 2835947520 | bytes 12142080 | tf_op jit(solution)/shard_map/dot_general | solution.py:50
  477.0 0.0 slice-start.1
  477.0 9.9 %convolution_bitcast_fusion.1 = f32[24,512,480]{1,2,0:T(8,128)} fusion(bf16[60,24,8,256]{3,2,1,0:T(8,128)(2,1)S(1)} %bitcast.81, f32[256,256]{1,0:T(8,128)S(1)} %get-tuple-element.27, f32[256,256]{1,0:T(8,128)S(1)} %get-tuple-element.28), kind=kOutput, calls=%fused_computation.18 | convolution fusion | flops 3020292096 | bytes 30015488 | tf_op jit(solution)/shard_map/vy,pyc->pvc/dot_general | solution.py:52
  486.9 11.4 %fusion.22 = f32[1,24,256,240]{2,3,1,0:T(8,128)} fusion(f32[24,512,480]{1,2,0:T(8,128)} %convolution_bitcast_fusion.1), kind=kLoop, calls=%fused_computation.36 | loop fusion | flops 7372800 | bytes 29491200 | tf_op jit(solution)/shard_map/reshape | solution.py:55
  498.3 0.0 slice-done
  498.3 0.0 slice-done.1
  498.3 8.0 %pad_maximum_fusion.2 = f32[2,24,256,240]{2,3,1,0:T(8,128)} fusion(f32[1,24,256,240]{2,3,1,0:T(8,128)S(1)} %bitcast.84, f32[1,24,256,240]{2,3,1,0:T(8,128)} %fusion.22), kind=kLoop, calls=%fused_computation.14 | loop fusion | flops 2949120 | bytes 23592960 | tf_op jit(solution)/shard_map/concatenate | solution.py:84
  (5 shorter events, 0.1 us)
Async XLA Ops:
  6.5 167.5 %reduce-scatter.5.cloned.1.call-start = ((), (), s32[]{:S(2)}) async-start(), calls=%async_computation.5 | async-start | bytes 18874368 | tf_op jit(solution)/shard_map/reduce_scatter | solution.py:74
  98.8 1.4 copy-start
  98.8 99.1 %reduce-scatter.3.cloned.1.call-start = ((), (), s32[]{:S(2)}) async-start(), calls=%async_computation.4 | async-start | bytes 18874368 | tf_op jit(solution)/shard_map/reduce_scatter | solution.py:74
  174.0 145.7 %all-to-all-start.1 = ((bf16[192,32,480]{2,1,0:T(8,128)(2,1)}), bf16[192,32,480]{2,1,0:T(8,128)(2,1)}, u32[]{:S(2)}, u32[]{:S(2)}) async-start(bf16[192,32,480]{2,1,0:T(8,128)(2,1)} %reduce-scatter.5.cloned.1.call-done), calls=%async_computation.3 | async-start | bytes 12582912 | tf_op jit(solution)/shard_map/all_to_all | solution.py:80
  319.7 142.1 %all-to-all-start = ((bf16[192,32,480]{2,1,0:T(8,128)(2,1)}), bf16[192,32,480]{2,1,0:T(8,128)(2,1)}, u32[]{:S(2)}, u32[]{:S(2)}) async-start(bf16[192,32,480]{2,1,0:T(8,128)(2,1)} %reduce-scatter.3.cloned.1.call-done), calls=%async_computation.1 | async-start | bytes 12582912 | tf_op jit(solution)/shard_map/all_to_all | solution.py:80
  468.3 29.9 %slice-start = ((s8[5898240]{0:T(1024)(128)(4,1)}), s8[4194304]{0:T(1024)(128)(4,1)S(1)}, s32[]{:S(2)}) async-start(s8[5898240]{0:T(1024)(128)(4,1)} %bitcast.83), calls=%async_computation.6 | async-start | bytes 8388608
  477.0 21.3 %slice-start.1 = ((s8[5898240]{0:T(1024)(128)(4,1)}), s8[1703936]{0:T(1024)(128)(4,1)S(1)}, s32[]{:S(2)}) async-start(s8[5898240]{0:T(1024)(128)(4,1)} %bitcast.83), calls=%async_computation.7 | async-start | bytes 3407872
Sparse Core Ops, SparseCore 0:
  99.0 23.4 reduce-scatter.4
  174.1 23.7 reduce-scatter.2
where the time goes:
time: 515 us; the launch traced here: 513 us
  waiting for transfers between devices  244 us (47%)
  matrix products  102 us (20%)
  other arithmetic  94.6 us (18%)
  local copies, waits for them, and re-layouts  46.4 us (9%)
  between operations  13.6 us (3%)
  starting transfers between devices  12.8 us (2%)
    all_to_all x2, waiting for transfers between devices, one_group(): lax.all_to_all(summed, 'space', split_axis=0, concat_axis=1, tiled=True)  227 us
    dot_general x2, matrix products, one_group(): jnp.dot(jnp.concatenate([coef_re, coef_im], 0), flat_s, preferred_element...  69.8 us
    optimization_barrier x2, local copies, waits for them, and re-layouts, one_group(): lax.optimization_barrier(jnp.concatenate([wave_re, wave_im], -1).astype(j...  33.4 us
    sub x2, other arithmetic, one_group(): wave_re = product[0, ..., :RX] - product[1, ..., RX:]  31.6 us
    reshape x2, other arithmetic, transform(): (spec_re * spec_re + spec_im * spec_im).reshape(count, per_device, RY, RX)  22.7 us
    dot_general x2, matrix products, transform(): jnp.einsum('vy,pyc->pvc', table_y, half, preferred_element_type=jnp.float32)  19.5 us
    reduce_scatter x2, waiting for transfers between devices, one_group(): lax.psum_scatter(rounded.astype(jnp.float32).astype(jnp.bfloat16), 'beam'...  16.3 us
    convert_element_type x1, other arithmetic, coefficients(): (scale * jnp.cos(theta)).astype(jnp.bfloat16)  16 us
  transfers between devices with their start and end apart: 4, of which 3 were waited for; matrix products, arithmetic and copies ran while one was open for 21% of the time, Pallas kernels for 0%

commit v1 on v0

--- a/solution.py
+++ b/solution.py
@@ -77,7 +77,12 @@
             scatter_dimension=0,
             tiled=True,
         )
-        wave = lax.all_to_all(summed, "space", split_axis=0, concat_axis=1, tiled=True)
+        wave = jnp.concatenate(
+            lax.all_to_all(
+                jnp.stack(jnp.split(summed, lax.axis_size("space"), axis=0)), "space", 0, 0
+            ),
+            axis=1,
+        )
         return transform(wave, count)
 
     outputs = [one_group(positions[batch : batch + 1]) for batch in range(n_batch)]

time: 515 us -> 533 us (1.035)
  local copies, waits for them, and re-layouts: 46.4 us -> 80.7 us
  waiting for transfers between devices: 244 us -> 227 us
    unnamed x6 -> x20, local copies, waits for them, and re-layouts: 1.16 us -> 31 us
    reduce_scatter x2, waiting for transfers between devices: 16.3 us -> 0.03 us  [one_group(): lax.psum_scatter(rounded.astype(jnp.float32).astype(jnp.bfloat16), 'beam'...]
    all_to_all x2 -> x0, local copies, waits for them, and re-layouts: 10 us -> none  [one_group(): lax.all_to_all(summed, 'space', split_axis=0, concat_axis=1, tiled=True)]
    reshape x0 -> x2, local copies, waits for them, and re-layouts: none -> 10 us  [one_group(): jnp.concatenate(lax.all_to_all(jnp.stack(jnp.split(summed, lax.axis_size(...]
  transfers between devices with their start and end apart: 4 -> 4, of which waited for: 3 -> 2; matrix products, arithmetic and copies ran while one was open for 21% -> 26% of each run, Pallas kernels for 0% -> 0%
where the time goes in v1:
time: 533 us; the launch traced here: 531 us
  waiting for transfers between devices  227 us (43%)
  matrix products  102 us (19%)
  other arithmetic  94.6 us (18%)
  local copies, waits for them, and re-layouts  80.7 us (15%)
  between operations  13.6 us (3%)
  starting transfers between devices  13 us (2%)
    all_to_all x2, waiting for transfers between devices, one_group(): lax.all_to_all(jnp.stack(jnp.split(summed, lax.axis_size('space'), axis=0...  227 us
    dot_general x2, matrix products, one_group(): jnp.dot(jnp.concatenate([coef_re, coef_im], 0), flat_s, preferred_element...  69.8 us
    optimization_barrier x2, local copies, waits for them, and re-layouts, one_group(): lax.optimization_barrier(jnp.concatenate([wave_re, wave_im], -1).astype(j...  33.4 us
    sub x2, other arithmetic, one_group(): wave_re = product[0, ..., :RX] - product[1, ..., RX:]  31.6 us
    unnamed x20, local copies, waits for them, and re-layouts  31 us
    reshape x2, other arithmetic, transform(): (spec_re * spec_re + spec_im * spec_im).reshape(count, per_device, RY, RX)  22.7 us
    dot_general x2, matrix products, transform(): jnp.einsum('vy,pyc->pvc', table_y, half, preferred_element_type=jnp.float32)  19.5 us
    convert_element_type x1, other arithmetic, coefficients(): (scale * jnp.cos(theta)).astype(jnp.bfloat16)  16 us
  transfers between devices with their start and end apart: 4, of which 2 were waited for; matrix products, arithmetic and copies ran while one was open for 26% of the time, Pallas kernels for 0%

profile of v1, /device:TPU:0, one launch (start us, length us, event | category | flops | bytes accessed | tf_op | source)
XLA Modules:
  0.0 530.7 jit_solution(6259875964393075119)
XLA Ops:
  6.5 0.7 broadcast_multiply_fusion
  7.2 0.7 fusion.87
  7.9 0.8 fusion.86
  8.7 0.1 reshape.52
  9.2 16.0 %multiply_convert_fusion.3 = (bf16[384,1024]{1,0:T(8,128)(2,1)S(1)}, bf16[384,1024]{1,0:T(8,128)(2,1)S(1)}, bf16[384,1024]{1,0:T(8,128)(2,1)S(1)}, bf16[384,1024]{1,0:T(8,128)(2,1)S(1)}) fusion(s32[1024]{0:T(1024)S(1)} %bitcast.152, s32[384]{0:T(512)S(1)} %get-tuple-element.6, s32[1024]{0:T(1024)S(1)} %bitcast.151, s32[384]{0:T(512)S(1)} %get-tuple-element.5, ...), kind=kLoop, calls=%fused_computation.75 | loop fusion | flops 23592960 | bytes 3168256 | tf_op jit(solution)/shard_map/convert_element_type | solution.py:34
  25.2 1.5 pad_maximum_fusion.3
  26.7 34.1 %fusion = f32[2,384,32,480]{1,3,2,0:T(8,128)} fusion(bf16[2,384,1024,1]{2,1,3,0:T(8,128)(2,1)S(1)} %bitcast.148, bf16[1024,32,480]{0,2,1:T(8,128)(2,1)} %param.5), kind=kOutput, calls=%fused_computation | convolution fusion | flops 24159191040 | bytes 80216064 | tf_op jit(solution)/shard_map/dot_general | solution.py:63
  60.7 15.8 %fusion.10 = (bf16[384,32,240]{0,2,1:T(8,128)(2,1)S(1)}, bf16[384,32,240]{0,2,1:T(8,128)(2,1)S(1)}) fusion(f32[2,384,32,480]{1,3,2,0:T(8,128)} %fusion), kind=kLoop, calls=%fused_computation.21 | loop fusion | flops 11796480 | bytes 58982400 | tf_op jit(solution)/shard_map/sub | solution.py:69
  76.6 5.5 %pad_maximum_fusion.1 = bf16[384,32,480]{0,2,1:T(8,128)(2,1)} fusion(bf16[384,32,240]{0,2,1:T(8,128)(2,1)S(1)} %get-tuple-element.12, bf16[384,32,240]{0,2,1:T(8,128)(2,1)S(1)} %get-tuple-element.11), kind=kLoop, calls=%fused_computation.13 | loop fusion | flops 23592960 | bytes 23592960 | tf_op jit(solution)/shard_map/concatenate | solution.py:72
  82.1 16.8 %copy.19 = bf16[384,32,480]{2,1,0:T(8,128)(2,1)} copy(bf16[384,32,480]{0,2,1:T(8,128)(2,1)} %pad_maximum_fusion.1) | data formatting | bytes 23592960 | tf_op jit(solution)/shard_map/optimization_barrier | solution.py:71
  98.8 0.2 reduce-scatter.3.cloned.1.call-start
  99.1 1.2 copy-done
  100.2 35.8 %fusion.2 = f32[2,384,32,480]{1,3,2,0:T(8,128)} fusion(bf16[2,384,1024,1]{2,1,3,0:T(8,128)(2,1)S(1)} %bitcast.147, bf16[1024,32,480]{0,2,1:T(8,128)(2,1)} %param.5), kind=kOutput, calls=%fused_computation.2 | convolution fusion | flops 24159191040 | bytes 80216064 | tf_op jit(solution)/shard_map/dot_general | solution.py:63
  136.0 15.8 %fusion.8 = (bf16[384,32,240]{0,2,1:T(8,128)(2,1)S(1)}, bf16[384,32,240]{0,2,1:T(8,128)(2,1)S(1)}) fusion(f32[2,384,32,480]{1,3,2,0:T(8,128)} %fusion.2), kind=kLoop, calls=%fused_computation.19 | loop fusion | flops 11796480 | bytes 58982400 | tf_op jit(solution)/shard_map/sub | solution.py:69
  151.8 5.5 %pad_maximum_fusion = bf16[384,32,480]{0,2,1:T(8,128)(2,1)} fusion(bf16[384,32,240]{0,2,1:T(8,128)(2,1)S(1)} %get-tuple-element.10, bf16[384,32,240]{0,2,1:T(8,128)(2,1)S(1)} %get-tuple-element.9), kind=kLoop, calls=%fused_computation.12 | loop fusion | flops 23592960 | bytes 23592960 | tf_op jit(solution)/shard_map/concatenate | solution.py:72
  157.3 16.6 %copy.15 = bf16[384,32,480]{2,1,0:T(8,128)(2,1)} copy(bf16[384,32,480]{0,2,1:T(8,128)(2,1)} %pad_maximum_fusion) | data formatting | bytes 23592960 | tf_op jit(solution)/shard_map/optimization_barrier | solution.py:71
  174.0 2.1 fusion.53
  176.1 2.1 fusion.52
  178.2 2.1 fusion.51
  180.3 2.1 fusion.50
  182.4 2.3 fusion.49
  184.7 2.1 fusion.48
  186.8 2.4 fusion.47
  189.1 2.4 fusion.46
  191.5 7.9 %all-to-all-start.1 = ((bf16[8,24,32,480]{3,2,1,0:T(8,128)(2,1)}), bf16[8,24,32,480]{3,2,1,0:T(8,128)(2,1)}, u32[]{:S(2)}, u32[]{:S(2)}) async-start(bf16[8,24,32,480]{3,2,1,0:T(8,128)(2,1)} %fusion.46), calls=%async_computation.3 | async-start | bytes 12582912 | tf_op jit(solution)/shard_map/all_to_all | solution.py:81
  199.4 2.1 fusion.61
  201.5 2.1 fusion.60
  203.6 2.1 fusion.59
  205.7 2.1 fusion.58
  207.8 2.1 fusion.57
  209.9 2.1 fusion.56
  212.0 2.1 fusion.55
  214.1 2.1 fusion.54
  216.2 121.0 %all-to-all-done.1 = bf16[8,24,32,480]{3,2,1,0:T(8,128)(2,1)} async-done(((bf16[8,24,32,480]{3,2,1,0:T(8,128)(2,1)}), bf16[8,24,32,480]{3,2,1,0:T(8,128)(2,1)}, u32[]{:S(2)}, u32[]{:S(2)}) %all-to-all-start.1) | async-done | bytes 5898272 | tf_op jit(solution)/shard_map/all_to_all | solution.py:81
  337.2 5.0 all-to-all-start
  342.1 1.0 fusion.75
  343.1 1.1 negate_convert_fusion
  344.2 1.0 fusion.76
  345.2 3.4 copy.20
  348.6 4.0 convolution_convert_fusion
  352.7 9.6 %convolution_bitcast_fusion = f32[24,512,480]{1,2,0:T(8,128)} fusion(bf16[60,24,8,256]{3,2,1,0:T(8,128)(2,1)S(1)} %bitcast.142, f32[256,256]{1,0:T(8,128)S(1)} %get-tuple-element.27, f32[256,256]{1,0:T(8,128)S(1)} %get-tuple-element.28), kind=kOutput, calls=%fused_computation.17 | convolution fusion | flops 3020292096 | bytes 30015488 | tf_op jit(solution)/shard_map/vy,pyc->pvc/dot_general | solution.py:52
  362.3 11.4 %fusion.18 = f32[1,24,256,240]{2,3,1,0:T(8,128)} fusion(f32[24,512,480]{1,2,0:T(8,128)} %convolution_bitcast_fusion), kind=kLoop, calls=%fused_computation.30 | loop fusion | flops 7372800 | bytes 29491200 | tf_op jit(solution)/shard_map/reshape | solution.py:55
  373.7 105.7 %all-to-all-done = bf16[8,24,32,480]{3,2,1,0:T(8,128)(2,1)} async-done(((bf16[8,24,32,480]{3,2,1,0:T(8,128)(2,1)}), bf16[8,24,32,480]{3,2,1,0:T(8,128)(2,1)}, u32[]{:S(2)}, u32[]{:S(2)}) %all-to-all-start) | async-done | bytes 5898272 | tf_op jit(solution)/shard_map/all_to_all | solution.py:81
  479.3 6.6 %copy.16 = bf16[24,8,32,480]{3,2,1,0:T(8,128)(2,1)} copy(bf16[24,8,32,480]{3,2,0,1:T(8,128)(2,1)} %bitcast.20) | data formatting | bytes 11796480 | tf_op jit(solution)/shard_map/reshape | solution.py:80
  485.9 8.7 %convolution_convert_fusion.1 = bf16[6144,480]{0,1:T(8,128)(2,1)S(1)} fusion(bf16[6144,480]{1,0:T(8,128)(2,1)} %bitcast.145, bf16[240,240]{1,0:T(8,128)(2,1)S(1)} %get-tuple-element.26, bf16[240,240]{1,0:T(8,128)(2,1)S(1)} %fusion.75, bf16[240,240]{1,0:T(8,128)(2,1)S(1)} %get-tuple-element.25), kind=kOutput, calls=%fused_computation.16 | convolution fusion | flops 2835947520 | bytes 12142080 | tf_op jit(solution)/shard_map/dot_general | solution.py:50
  494.6 9.9 %convolution_bitcast_fusion.1 = f32[24,512,480]{1,2,0:T(8,128)} fusion(bf16[60,24,8,256]{3,2,1,0:T(8,128)(2,1)S(1)} %bitcast.141, f32[256,256]{1,0:T(8,128)S(1)} %get-tuple-element.27, f32[256,256]{1,0:T(8,128)S(1)} %get-tuple-element.28), kind=kOutput, calls=%fused_computation.18 | convolution fusion | flops 3020292096 | bytes 30015488 | tf_op jit(solution)/shard_map/vy,pyc->pvc/dot_general | solution.py:52
  504.5 11.4 %fusion.22 = f32[1,24,256,240]{2,3,1,0:T(8,128)} fusion(f32[24,512,480]{1,2,0:T(8,128)} %convolution_bitcast_fusion.1), kind=kLoop, calls=%fused_computation.36 | loop fusion | flops 7372800 | bytes 29491200 | tf_op jit(solution)/shard_map/reshape | solution.py:55
  515.9 8.0 %pad_maximum_fusion.2 = f32[2,24,256,240]{2,3,1,0:T(8,128)} fusion(f32[1,24,256,240]{2,3,1,0:T(8,128)S(1)} %bitcast.144, f32[1,24,256,240]{2,3,1,0:T(8,128)} %fusion.22), kind=kLoop, calls=%fused_computation.14 | loop fusion | flops 2949120 | bytes 23592960 | tf_op jit(solution)/shard_map/concatenate | solution.py:89
  (18 shorter events, 0.4 us)
Async XLA Ops:
  6.5 167.5 %reduce-scatter.5.cloned.1.call-start = ((), (), s32[]{:S(2)}) async-start(), calls=%async_computation.5 | async-start | bytes 18874368 | tf_op jit(solution)/shard_map/reduce_scatter | solution.py:74
  98.8 1.4 copy-start
  98.8 100.5 %reduce-scatter.3.cloned.1.call-start = ((), (), s32[]{:S(2)}) async-start(), calls=%async_computation.4 | async-start | bytes 18874368 | tf_op jit(solution)/shard_map/reduce_scatter | solution.py:74
  191.5 145.7 %all-to-all-start.1 = ((bf16[8,24,32,480]{3,2,1,0:T(8,128)(2,1)}), bf16[8,24,32,480]{3,2,1,0:T(8,128)(2,1)}, u32[]{:S(2)}, u32[]{:S(2)}) async-start(bf16[8,24,32,480]{3,2,1,0:T(8,128)(2,1)} %fusion.46), calls=%async_computation.3 | async-start | bytes 12582912 | tf_op jit(solution)/shard_map/all_to_all | solution.py:81
  337.2 142.1 %all-to-all-start = ((bf16[8,24,32,480]{3,2,1,0:T(8,128)(2,1)}), bf16[8,24,32,480]{3,2,1,0:T(8,128)(2,1)}, u32[]{:S(2)}, u32[]{:S(2)}) async-start(bf16[8,24,32,480]{3,2,1,0:T(8,128)(2,1)} %fusion.54), calls=%async_computation.1 | async-start | bytes 12582912 | tf_op jit(solution)/shard_map/all_to_all | solution.py:81
  485.9 29.9 %slice-start = ((s8[5898240]{0:T(1024)(128)(4,1)}), s8[4194304]{0:T(1024)(128)(4,1)S(1)}, s32[]{:S(2)}) async-start(s8[5898240]{0:T(1024)(128)(4,1)} %bitcast.143), calls=%async_computation.6 | async-start | bytes 8388608
  494.6 21.3 %slice-start.1 = ((s8[5898240]{0:T(1024)(128)(4,1)}), s8[1703936]{0:T(1024)(128)(4,1)S(1)}, s32[]{:S(2)}) async-start(s8[5898240]{0:T(1024)(128)(4,1)} %bitcast.143), calls=%async_computation.7 | async-start | bytes 3407872
Sparse Core Ops, SparseCore 0:
  99.0 23.4 reduce-scatter.4
  174.1 23.7 reduce-scatter.2
